TPU v7x, 32 devices: a whole 2x2x4 slice. The times are simulated.
32 devices in a mesh: lat: 8 (over z, y), lev: 4 (over x, core).
Axes of the slice: x: 2, y: 2, z: 4, core: 2. Of those that a mesh axis runs over, the one named last changes fastest.
Arguments:
- tracer: float32 [2, 4, 384, 1152], P(None, 'lev', 'lat'), may hold values from 0.1 to 2
- east_courant: float32 [4, 384, 1152], P('lev', 'lat'), may hold values from -0.8 to 0.8
- north_courant: float32 [4, 384, 1152], P('lev', 'lat'), may hold values from -0.8 to 0.8
- fall_speed: float32 [2, 4, 384, 1152], P(None, 'lev', 'lat'), may hold values from 0.05 to 0.6
Outputs:
- tracer_out: float32 [2, 4, 384, 1152], P(None, 'lev', 'lat')
- deposit: float32 [2, 384, 1152], P(None, 'lat', 'lev')
All inputs are finite; a program needn't handle non-finite values.
Results may differ from a plain program's by a relative error of at most 0.0003.
Values sent between devices are 32-bit elements; how exact they have to be, the bound alone decides.
No kernel may reach another device: no remote copies, remote signals or barrier semaphores. Data moves between devices by JAX's collectives and lax.ppermute only.
A program may use at most 64 MiB of HBM per device.

v0:
```python
import jax
import jax.numpy as jnp
from jax import lax
from jax.sharding import PartitionSpec as P

HSUB = 4
SETTLE_SUBSTEPS = 6


def passed_along(block, axis, distance):
    devices = range(lax.axis_size(axis))
    route = [(i - distance, i) for i in devices if i - distance in devices]
    return lax.ppermute(block, axis, route)


def extended(block, sides, width):
    for axis, dim in sides:
        count = lax.axis_size(axis)
        forward = [(i, i + 1) for i in range(count - 1)]
        backward = [(target, source) for source, target in forward]
        low = lax.ppermute(
            lax.slice_in_dim(block, block.shape[dim] - width, None, axis=dim), axis, forward
        )
        high = lax.ppermute(lax.slice_in_dim(block, 0, width, axis=dim), axis, backward)
        block = jnp.concatenate([low, block, high], axis=dim)
    return block


def limiter_face_value(outer_west, inner_west, inner_east, outer_east):
    interp = 7.0 / 12.0 * (inner_west + inner_east) - 1.0 / 12.0 * (outer_west + outer_east)
    return jnp.clip(
        interp, jnp.minimum(inner_west, inner_east), jnp.maximum(inner_west, inner_east)
    )


def window_for_cell(source, start, length, axis_dim):
    return lax.slice_in_dim(source, start, start + length, axis=axis_dim)


def sweep(halo_padded_field, courant, axis_dim):
    cells = halo_padded_field.shape[axis_dim] - 6
    faces = limiter_face_value(
        window_for_cell(halo_padded_field, 0, cells + 3, axis_dim),
        window_for_cell(halo_padded_field, 1, cells + 3, axis_dim),
        window_for_cell(halo_padded_field, 2, cells + 3, axis_dim),
        window_for_cell(halo_padded_field, 3, cells + 3, axis_dim),
    )
    middle = window_for_cell(halo_padded_field, 2, cells + 2, axis_dim)
    west_face = window_for_cell(faces, 0, cells + 2, axis_dim)
    east_face = window_for_cell(faces, 1, cells + 2, axis_dim)
    spread = east_face - west_face
    curvature = 6.0 * middle - 3.0 * (west_face + east_face)
    courant_abs = jnp.abs(courant)
    shape_term = 1.0 - 2.0 / 3.0 * courant_abs
    from_west = window_for_cell(east_face, 0, cells + 1, axis_dim) - 0.5 * courant_abs * (
        window_for_cell(spread, 0, cells + 1, axis_dim)
        - shape_term * window_for_cell(curvature, 0, cells + 1, axis_dim)
    )
    from_east = window_for_cell(west_face, 1, cells + 1, axis_dim) + 0.5 * courant_abs * (
        window_for_cell(spread, 1, cells + 1, axis_dim)
        + shape_term * window_for_cell(curvature, 1, cells + 1, axis_dim)
    )
    face_flux_values = courant * jnp.where(courant >= 0, from_west, from_east)
    return window_for_cell(halo_padded_field, 3, cells, axis_dim) - (
        window_for_cell(face_flux_values, 1, cells, axis_dim)
        - window_for_cell(face_flux_values, 0, cells, axis_dim)
    )


def zonal(field, east_courant):
    last_dim = field.ndim - 1
    width = field.shape[last_dim]
    halo_padded_field = jnp.concatenate(
        [
            window_for_cell(field, width - 3, 3, last_dim),
            field,
            window_for_cell(field, 0, 3, last_dim),
        ],
        last_dim,
    )
    cour_dim = east_courant.ndim - 1
    courant = jnp.concatenate(
        [window_for_cell(east_courant, width - 1, 1, cour_dim), east_courant], cour_dim
    )
    return sweep(halo_padded_field, courant, last_dim)


def settle_flat(column_mass, fall_speed):
    deposit = jnp.zeros_like(column_mass[:, 0])
    for settle_substep in range(SETTLE_SUBSTEPS):
        speeds = fall_speed * (1.0 + 0.5 * jnp.tanh(column_mass))
        face_flux_values = speeds * column_mass
        inflow = jnp.concatenate(
            [jnp.zeros_like(face_flux_values[:, :1]), face_flux_values[:, :-1]], 1
        )
        column_mass = column_mass + inflow - face_flux_values
        deposit = deposit + face_flux_values[:, -1]
    return (column_mass, deposit)


def columns_settle(split_portions):
    column_mass, speed_piece = split_portions
    shape_full = column_mass.shape
    flat_shape = (shape_full[0], shape_full[1], shape_full[2] * shape_full[3])
    settled, deposit = settle_flat(column_mass.reshape(flat_shape), speed_piece.reshape(flat_shape))
    returned = lax.all_to_all(
        settled.reshape(shape_full), "lev", split_axis=1, concat_axis=3, tiled=True
    )
    return (returned, deposit.reshape((shape_full[0], shape_full[2], shape_full[3])))


def on_device(tracer, east_courant, north_courant, fall_speed):
    band_rows = tracer.shape[2]
    all_rows = band_rows * lax.axis_size("lat")
    first_row = lax.axis_index("lat") * band_rows
    row_ids = first_row + jnp.arange(band_rows, dtype=jnp.int32)
    north_faces = jnp.where(
        (row_ids == all_rows - 1)[None, :, None], jnp.zeros_like(north_courant), north_courant
    )
    southern_row = passed_along(north_faces[:, band_rows - 1 :, :], "lat", 1)
    face_cour = jnp.concatenate([southern_row, north_faces], 1)
    field = tracer
    for settle_substep in range(HSUB):
        field = zonal(field, east_courant)
        halo_padded_field = extended(field, (("lat", 2),), 3)
        field = sweep(halo_padded_field, face_cour, 2)
    field, deposit = columns_settle(
        (
            lax.all_to_all(field, "lev", split_axis=3, concat_axis=1, tiled=True),
            lax.all_to_all(fall_speed, "lev", split_axis=3, concat_axis=1, tiled=True),
        )
    )
    field = zonal(field, east_courant)
    halo_padded_field = extended(field, (("lat", 2),), 3)
    field = sweep(halo_padded_field, face_cour, 2)
    return (field, deposit)


def solution(mesh):
    in_specs = (
        P(None, "lev", "lat", None),
        P("lev", "lat", None),
        P("lev", "lat", None),
        P(None, "lev", "lat", None),
    )
    out_specs = (P(None, "lev", "lat", None), P(None, "lat", "lev"))
    return jax.shard_map(
        on_device, mesh=mesh, in_specs=in_specs, out_specs=out_specs, check_vma=False
    )
```

profile of v0, /device:TPU:0, one launch (start us, length us, event | category | flops | bytes accessed | tf_op | source)
XLA Modules:
  0.0 129.7 jit_solution(10379016936662951680)
XLA Ops:
  1.8 4.9 %collective-permute-start = (f32[1,1,1152]{2,1,0:T(1,128)S(1)}, f32[1,1,1152]{2,1,0:T(1,128)S(1)}, u32[]{:S(2)}, u32[]{:S(2)}) collective-permute-start(f32[1,1,1152]{2,1,0:T(1,128)S(1)} %slice.702), channel_id=1, source_target_pairs={{0,4},{4,8},{8,12},{12,16},{16,20},{20,24},{24,28},{1,5},{5,9},{9,... | collective-permute-start | bytes 13832 | tf_op jit(solution)/shard_map/ppermute | solution.py:13
  11.7 3.4 %collective-permute-start.1 = (f32[2,1,3,1152]{3,2,1,0:T(4,128)S(1)}, f32[2,1,3,1152]{3,2,1,0:T(4,128)S(1)}, u32[]{:S(2)}, u32[]{:S(2)}) collective-permute-start(f32[2,1,3,1152]{3,2,1,0:T(4,128)S(1)} %get-tuple-element.46), channel_id=1, source_target_pairs={{0,4},{4,8},{8,12},{12,16},{16,20},{20,24},{24,28},{1,5},{5,9},{9,... | collective-permute-start | bytes 82952 | tf_op jit(solution)/shard_map/ppermute | solution.py:21
  15.1 1.3 collective-permute-start.2
  16.7 4.2 %collective-permute-done.2 = f32[2,1,3,1152]{3,2,1,0:T(4,128)S(1)} collective-permute-done((f32[2,1,3,1152]{3,2,1,0:T(4,128)S(1)}, f32[2,1,3,1152]{3,2,1,0:T(4,128)S(1)}, u32[]{:S(2)}, u32[]{:S(2)}) %collective-permute-start.2) | collective-permute-done | bytes 27680 | tf_op jit(solution)/shard_map/ppermute | solution.py:24
  23.7 4.3 %collective-permute-start.3 = (f32[2,1,3,1152]{3,2,1,0:T(4,128)S(1)}, f32[2,1,3,1152]{3,2,1,0:T(4,128)S(1)}, u32[]{:S(2)}, u32[]{:S(2)}) collective-permute-start(f32[2,1,3,1152]{3,2,1,0:T(4,128)S(1)} %get-tuple-element.42), channel_id=1, source_target_pairs={{0,4},{4,8},{8,12},{12,16},{16,20},{20,24},{24,28},{1,5},{5,9},{9,... | collective-permute-start | bytes 82952 | tf_op jit(solution)/shard_map/ppermute | solution.py:21
  28.0 1.3 collective-permute-start.4
  29.6 4.2 %collective-permute-done.4 = f32[2,1,3,1152]{3,2,1,0:T(4,128)S(1)} collective-permute-done((f32[2,1,3,1152]{3,2,1,0:T(4,128)S(1)}, f32[2,1,3,1152]{3,2,1,0:T(4,128)S(1)}, u32[]{:S(2)}, u32[]{:S(2)}) %collective-permute-start.4) | collective-permute-done | bytes 27680 | tf_op jit(solution)/shard_map/ppermute | solution.py:24
  36.6 3.4 %collective-permute-start.5 = (f32[2,1,3,1152]{3,2,1,0:T(4,128)S(1)}, f32[2,1,3,1152]{3,2,1,0:T(4,128)S(1)}, u32[]{:S(2)}, u32[]{:S(2)}) collective-permute-start(f32[2,1,3,1152]{3,2,1,0:T(4,128)S(1)} %get-tuple-element.38), channel_id=1, source_target_pairs={{0,4},{4,8},{8,12},{12,16},{16,20},{20,24},{24,28},{1,5},{5,9},{9,... | collective-permute-start | bytes 82952 | tf_op jit(solution)/shard_map/ppermute | solution.py:21
  40.0 1.3 collective-permute-start.6
  41.8 4.1 %collective-permute-done.6 = f32[2,1,3,1152]{3,2,1,0:T(4,128)S(1)} collective-permute-done((f32[2,1,3,1152]{3,2,1,0:T(4,128)S(1)}, f32[2,1,3,1152]{3,2,1,0:T(4,128)S(1)}, u32[]{:S(2)}, u32[]{:S(2)}) %collective-permute-start.6) | collective-permute-done | bytes 27680 | tf_op jit(solution)/shard_map/ppermute | solution.py:24
  48.6 4.3 %collective-permute-start.7 = (f32[2,1,3,1152]{3,2,1,0:T(4,128)S(1)}, f32[2,1,3,1152]{3,2,1,0:T(4,128)S(1)}, u32[]{:S(2)}, u32[]{:S(2)}) collective-permute-start(f32[2,1,3,1152]{3,2,1,0:T(4,128)S(1)} %get-tuple-element.34), channel_id=1, source_target_pairs={{0,4},{4,8},{8,12},{12,16},{16,20},{20,24},{24,28},{1,5},{5,9},{9,... | collective-permute-start | bytes 82952 | tf_op jit(solution)/shard_map/ppermute | solution.py:21
  52.9 1.5 %collective-permute-start.8 = (f32[2,1,3,1152]{3,2,1,0:T(4,128)S(1)}, f32[2,1,3,1152]{3,2,1,0:T(4,128)S(1)}, u32[]{:S(2)}, u32[]{:S(2)}) collective-permute-start(f32[2,1,3,1152]{3,2,1,0:T(4,128)S(1)} %get-tuple-element.35), channel_id=1, source_target_pairs={{4,0},{8,4},{12,8},{16,12},{20,16},{24,20},{28,24},{5,1},{9,5},{13... | collective-permute-start | bytes 82952 | tf_op jit(solution)/shard_map/ppermute | solution.py:24
  54.4 2.0 %copy.56 = f32[2,1,48,1152]{2,0,1,3:T(2,128)S(1)} copy(f32[2,1,48,1152]{3,2,1,0:T(8,128)} %param.7) | data formatting | bytes 884736 | tf_op args[3]
  56.4 2.9 %reshape.594 = f32[4,1,27648]{2,1,0:T(1,128)} reshape(f32[1152,1,2,48]{3,2,1,0:T(2,128)S(1)} %bitcast.40) | data formatting | bytes 884736
  59.3 4.1 %all-to-all-start.1 = ((f32[4,1,27648]{2,1,0:T(1,128)}), f32[4,1,27648]{2,1,0:T(1,128)}, u32[]{:S(2)}, u32[]{:S(2)}) async-start(f32[4,1,27648]{2,1,0:T(1,128)} %reshape.594), calls=%async_computation.1 | async-start | bytes 884736 | tf_op jit(solution)/shard_map/all_to_all | solution.py:130
  65.4 2.8 %reshape.596 = f32[4,1,27648]{2,1,0:T(1,128)} reshape(f32[1152,1,2,48]{3,2,1,0:T(2,128)S(1)} %bitcast.37) | data formatting | bytes 884736
  68.3 3.1 %all-to-all-done.1 = f32[4,1,27648]{2,1,0:T(1,128)} async-done(((f32[4,1,27648]{2,1,0:T(1,128)}), f32[4,1,27648]{2,1,0:T(1,128)}, u32[]{:S(2)}, u32[]{:S(2)}) %all-to-all-start.1) | async-done | bytes 442400 | tf_op jit(solution)/shard_map/all_to_all | solution.py:130
  71.4 4.1 %all-to-all-start = ((f32[4,1,27648]{2,1,0:T(1,128)}), f32[4,1,27648]{2,1,0:T(1,128)}, u32[]{:S(2)}, u32[]{:S(2)}) async-start(f32[4,1,27648]{2,1,0:T(1,128)} %reshape.596), calls=%async_computation | async-start | bytes 884736 | tf_op jit(solution)/shard_map/all_to_all | solution.py:129
  76.0 2.8 %reduce.2 = f32[4,27648]{1,0:T(4,128)S(1)} reduce(f32[4,1,27648]{2,1,0:T(1,128)} %all-to-all-done.1, f32[]{:T(128)} %broadcast.305), dimensions={1}, to_apply=%all_to_all.38.reduce_sub_computation | reduce | bytes 884740 | tf_op jit(solution)/shard_map/all_to_all | solution.py:130
  78.8 1.9 %reshape.595 = f32[1152,1,2,48]{3,2,1,0:T(2,128)S(1)} reshape(f32[4,27648]{1,0:T(4,128)S(1)} %reduce.2) | data formatting | bytes 884736
  81.8 1.7 %all-to-all-done = f32[4,1,27648]{2,1,0:T(1,128)} async-done(((f32[4,1,27648]{2,1,0:T(1,128)}), f32[4,1,27648]{2,1,0:T(1,128)}, u32[]{:S(2)}, u32[]{:S(2)}) %all-to-all-start) | async-done | bytes 442400 | tf_op jit(solution)/shard_map/all_to_all | solution.py:129
  83.5 3.6 %reduce.3 = f32[4,27648]{1,0:T(4,128)} reduce(f32[4,1,27648]{2,1,0:T(1,128)} %all-to-all-done, f32[]{:T(128)} %broadcast.305), dimensions={1}, to_apply=%all_to_all.35.reduce_sub_computation | reduce | bytes 884740 | tf_op jit(solution)/shard_map/all_to_all | solution.py:129
  87.1 2.9 %reshape.597 = f32[1152,1,2,48]{3,2,1,0:T(2,128)S(1)} reshape(f32[4,27648]{1,0:T(4,128)} %reduce.3) | data formatting | bytes 884736
  90.0 1.3 %copy.55 = f32[2,1,48,4,288]{4,2,3,0,1:T(8,128)} copy(f32[2,1,48,4,288]{2,0,4,3,1:T(2,128)S(1)} %bitcast.39) | data formatting | bytes 884736 | tf_op jit(solution)/shard_map/all_to_all | solution.py:129
  91.4 1.5 %reshape.589 = f32[2,4,13824]{2,1,0:T(4,128)S(1)} reshape(f32[2,4,1,48,288]{4,3,1,0,2:T(8,128)} %bitcast.48) | data formatting | bytes 884736 | tf_op jit(solution)/shard_map/reshape | solution.py:105
  96.7 1.3 %add_subtract_fusion = f32[2,4,13824]{2,1,0:T(4,128)} fusion(f32[2,3,13824]{2,1,0:T(4,128)S(1)} %bitcast.52, f32[2,4,13824]{2,1,0:T(4,128)S(1)} %get-tuple-element.7, f32[2,3,13824]{2,1,0:T(4,128)S(1)} %bitcast.46, f32[2,4,13824]{2,1,0:T(4,128)S(1)} %reshape.590), kind=kLoop, calls=%fused_computation.205 | loop fusion | flops 1327104 | bytes 1990656 | tf_op jit(solution)/shard_map/sub | solution.py:96
  98.0 2.3 %reshape.591 = f32[2,4,48,288]{3,2,1,0:T(8,128)} reshape(f32[2,4,13824]{2,1,0:T(4,128)} %add_subtract_fusion) | data formatting | bytes 884736 | tf_op jit(solution)/shard_map/reshape | solution.py:107
  101.4 11.9 %all_to_all.48 = f32[2,4,48,288]{3,2,0,1:T(8,128)S(1)} all-to-all(f32[2,4,48,288]{3,2,0,1:T(8,128)S(1)} %copy.58), channel_id=1, replica_groups=mesh['lat'=8,'lev'=4] {'lev'}, dimensions={1} | all-to-all | bytes 884736 | tf_op jit(solution)/shard_map/all_to_all | solution.py:106
  114.5 1.4 %all_to_all.44 = f32[2,1,48,1152]{3,2,1,0:T(8,128)S(1)} reshape(f32[2,1,48,4,288]{4,3,2,0,1:T(4,128)} %copy.59) | data formatting | bytes 884736 | tf_op jit(solution)/shard_map/all_to_all | solution.py:106
  117.7 4.5 %collective-permute-start.9 = (f32[2,1,3,1152]{3,2,1,0:T(4,128)S(1)}, f32[2,1,3,1152]{3,2,1,0:T(4,128)S(1)}, u32[]{:S(2)}, u32[]{:S(2)}) collective-permute-start(f32[2,1,3,1152]{3,2,1,0:T(4,128)S(1)} %get-tuple-element.30), channel_id=1, source_target_pairs={{0,4},{4,8},{8,12},{12,16},{16,20},{20,24},{24,28},{1,5},{5,9},{9,... | collective-permute-start | bytes 82952 | tf_op jit(solution)/shard_map/ppermute | solution.py:21
  123.5 2.3 %fusion.142 = f32[2,13824]{1,0:T(2,128)S(1)} fusion(f32[2,4,13824]{2,1,0:T(4,128)} %copy-done.4, f32[2,4,13824]{2,1,0:T(4,128)} %copy-done, f32[2,4,13824]{2,1,0:T(4,128)} %copy-done.3, f32[2,4,13824]{2,1,0:T(4,128)S(1)} %get-tuple-element.8, f32[2,4,13824]{2,1,0:T(4,128)} %copy-done.2, f32[2,4,13824]{2,1,0:T(4,128)S(1)} %multiply_multiply_fusion.5), kind=kLoop, calls=%fused_computation.228 | loop fusion | flops 138240 | bytes 774144 | tf_op jit(solution)/shard_map/add | solution.py:97
  126.7 1.4 %collective-permute-done.10 = f32[2,1,3,1152]{3,2,1,0:T(4,128)S(1)} collective-permute-done((f32[2,1,3,1152]{3,2,1,0:T(4,128)S(1)}, f32[2,1,3,1152]{3,2,1,0:T(4,128)S(1)}, u32[]{:S(2)}, u32[]{:S(2)}) %collective-permute-start.10) | collective-permute-done | bytes 27680 | tf_op jit(solution)/shard_map/ppermute | solution.py:24
  (106 shorter events, 30.3 us)
Async XLA Ops:
  0.6 9.1 %copy-start.5 = (f32[1,48,1152]{2,1,0:T(8,128)S(1)}, f32[1,48,1152]{2,1,0:T(8,128)}, u32[]{:S(2)}) copy-start(f32[1,48,1152]{2,1,0:T(8,128)} %param.5) | copy-start | bytes 663556
  0.6 9.0 %copy-start.1 = (f32[2,1,48,1152]{3,2,1,0:T(8,128)S(1)}, f32[2,1,48,1152]{3,2,1,0:T(8,128)}, u32[]{:S(2)}) copy-start(f32[2,1,48,1152]{3,2,1,0:T(8,128)} %param.4) | copy-start | bytes 1327108
  1.8 14.7 %collective-permute-start = (f32[1,1,1152]{2,1,0:T(1,128)S(1)}, f32[1,1,1152]{2,1,0:T(1,128)S(1)}, u32[]{:S(2)}, u32[]{:S(2)}) collective-permute-start(f32[1,1,1152]{2,1,0:T(1,128)S(1)} %slice.702), channel_id=1, source_target_pairs={{0,4},{4,8},{8,12},{12,16},{16,20},{20,24},{24,28},{1,5},{5,9},{9,... | collective-permute-start | bytes 13832 | tf_op jit(solution)/shard_map/ppermute | solution.py:13
  11.4 5.0 %copy-start.6 = (f32[1,48,1152]{2,1,0:T(8,128)S(1)}, f32[1,48,1152]{2,1,0:T(8,128)}, u32[]{:S(2)}) copy-start(f32[1,48,1152]{2,1,0:T(8,128)} %param.6) | copy-start | bytes 663556
  11.7 5.1 %collective-permute-start.1 = (f32[2,1,3,1152]{3,2,1,0:T(4,128)S(1)}, f32[2,1,3,1152]{3,2,1,0:T(4,128)S(1)}, u32[]{:S(2)}, u32[]{:S(2)}) collective-permute-start(f32[2,1,3,1152]{3,2,1,0:T(4,128)S(1)} %get-tuple-element.46), channel_id=1, source_target_pairs={{0,4},{4,8},{8,12},{12,16},{16,20},{20,24},{24,28},{1,5},{5,9},{9,... | collective-permute-start | bytes 82952 | tf_op jit(solution)/shard_map/ppermute | solution.py:21
  15.1 5.9 %collective-permute-start.2 = (f32[2,1,3,1152]{3,2,1,0:T(4,128)S(1)}, f32[2,1,3,1152]{3,2,1,0:T(4,128)S(1)}, u32[]{:S(2)}, u32[]{:S(2)}) collective-permute-start(f32[2,1,3,1152]{3,2,1,0:T(4,128)S(1)} %get-tuple-element.47), channel_id=1, source_target_pairs={{4,0},{8,4},{12,8},{16,12},{20,16},{24,20},{28,24},{5,1},{9,5},{13... | collective-permute-start | bytes 82952 | tf_op jit(solution)/shard_map/ppermute | solution.py:24
  23.7 6.0 %collective-permute-start.3 = (f32[2,1,3,1152]{3,2,1,0:T(4,128)S(1)}, f32[2,1,3,1152]{3,2,1,0:T(4,128)S(1)}, u32[]{:S(2)}, u32[]{:S(2)}) collective-permute-start(f32[2,1,3,1152]{3,2,1,0:T(4,128)S(1)} %get-tuple-element.42), channel_id=1, source_target_pairs={{0,4},{4,8},{8,12},{12,16},{16,20},{20,24},{24,28},{1,5},{5,9},{9,... | collective-permute-start | bytes 82952 | tf_op jit(solution)/shard_map/ppermute | solution.py:21
  28.0 5.9 %collective-permute-start.4 = (f32[2,1,3,1152]{3,2,1,0:T(4,128)S(1)}, f32[2,1,3,1152]{3,2,1,0:T(4,128)S(1)}, u32[]{:S(2)}, u32[]{:S(2)}) collective-permute-start(f32[2,1,3,1152]{3,2,1,0:T(4,128)S(1)} %get-tuple-element.43), channel_id=1, source_target_pairs={{4,0},{8,4},{12,8},{16,12},{20,16},{24,20},{28,24},{5,1},{9,5},{13... | collective-permute-start | bytes 82952 | tf_op jit(solution)/shard_map/ppermute | solution.py:24
  36.6 5.2 %collective-permute-start.5 = (f32[2,1,3,1152]{3,2,1,0:T(4,128)S(1)}, f32[2,1,3,1152]{3,2,1,0:T(4,128)S(1)}, u32[]{:S(2)}, u32[]{:S(2)}) collective-permute-start(f32[2,1,3,1152]{3,2,1,0:T(4,128)S(1)} %get-tuple-element.38), channel_id=1, source_target_pairs={{0,4},{4,8},{8,12},{12,16},{16,20},{20,24},{24,28},{1,5},{5,9},{9,... | collective-permute-start | bytes 82952 | tf_op jit(solution)/shard_map/ppermute | solution.py:21
  40.0 5.9 %collective-permute-start.6 = (f32[2,1,3,1152]{3,2,1,0:T(4,128)S(1)}, f32[2,1,3,1152]{3,2,1,0:T(4,128)S(1)}, u32[]{:S(2)}, u32[]{:S(2)}) collective-permute-start(f32[2,1,3,1152]{3,2,1,0:T(4,128)S(1)} %get-tuple-element.39), channel_id=1, source_target_pairs={{4,0},{8,4},{12,8},{16,12},{20,16},{24,20},{28,24},{5,1},{9,5},{13... | collective-permute-start | bytes 82952 | tf_op jit(solution)/shard_map/ppermute | solution.py:24
  48.6 14.8 %collective-permute-start.7 = (f32[2,1,3,1152]{3,2,1,0:T(4,128)S(1)}, f32[2,1,3,1152]{3,2,1,0:T(4,128)S(1)}, u32[]{:S(2)}, u32[]{:S(2)}) collective-permute-start(f32[2,1,3,1152]{3,2,1,0:T(4,128)S(1)} %get-tuple-element.34), channel_id=1, source_target_pairs={{0,4},{4,8},{8,12},{12,16},{16,20},{20,24},{24,28},{1,5},{5,9},{9,... | collective-permute-start | bytes 82952 | tf_op jit(solution)/shard_map/ppermute | solution.py:21
  52.9 10.5 %collective-permute-start.8 = (f32[2,1,3,1152]{3,2,1,0:T(4,128)S(1)}, f32[2,1,3,1152]{3,2,1,0:T(4,128)S(1)}, u32[]{:S(2)}, u32[]{:S(2)}) collective-permute-start(f32[2,1,3,1152]{3,2,1,0:T(4,128)S(1)} %get-tuple-element.35), channel_id=1, source_target_pairs={{4,0},{8,4},{12,8},{16,12},{20,16},{24,20},{28,24},{5,1},{9,5},{13... | collective-permute-start | bytes 82952 | tf_op jit(solution)/shard_map/ppermute | solution.py:24
  59.3 12.1 %all-to-all-start.1 = ((f32[4,1,27648]{2,1,0:T(1,128)}), f32[4,1,27648]{2,1,0:T(1,128)}, u32[]{:S(2)}, u32[]{:S(2)}) async-start(f32[4,1,27648]{2,1,0:T(1,128)} %reshape.594), calls=%async_computation.1 | async-start | bytes 884736 | tf_op jit(solution)/shard_map/all_to_all | solution.py:130
  71.4 12.1 %all-to-all-start = ((f32[4,1,27648]{2,1,0:T(1,128)}), f32[4,1,27648]{2,1,0:T(1,128)}, u32[]{:S(2)}, u32[]{:S(2)}) async-start(f32[4,1,27648]{2,1,0:T(1,128)} %reshape.596), calls=%async_computation | async-start | bytes 884736 | tf_op jit(solution)/shard_map/all_to_all | solution.py:129
  93.5 0.8 copy-start.2
  94.7 0.8 copy-start.3
  95.5 2.6 %copy-start = (f32[2,4,13824]{2,1,0:T(4,128)}, f32[2,4,13824]{2,1,0:T(4,128)S(1)}, u32[]{:S(2)}) copy-start(f32[2,4,13824]{2,1,0:T(4,128)S(1)} %get-tuple-element.6) | copy-start | bytes 1327108
  95.9 0.8 copy-start.4
  117.7 9.0 %collective-permute-start.9 = (f32[2,1,3,1152]{3,2,1,0:T(4,128)S(1)}, f32[2,1,3,1152]{3,2,1,0:T(4,128)S(1)}, u32[]{:S(2)}, u32[]{:S(2)}) collective-permute-start(f32[2,1,3,1152]{3,2,1,0:T(4,128)S(1)} %get-tuple-element.30), channel_id=1, source_target_pairs={{0,4},{4,8},{8,12},{12,16},{16,20},{20,24},{24,28},{1,5},{5,9},{9,... | collective-permute-start | bytes 82952 | tf_op jit(solution)/shard_map/ppermute | solution.py:21
  122.2 5.9 %collective-permute-start.10 = (f32[2,1,3,1152]{3,2,1,0:T(4,128)S(1)}, f32[2,1,3,1152]{3,2,1,0:T(4,128)S(1)}, u32[]{:S(2)}, u32[]{:S(2)}) collective-permute-start(f32[2,1,3,1152]{3,2,1,0:T(4,128)S(1)} %get-tuple-element.31), channel_id=1, source_target_pairs={{4,0},{8,4},{12,8},{16,12},{20,16},{24,20},{28,24},{5,1},{9,5},{13... | collective-permute-start | bytes 82952 | tf_op jit(solution)/shard_map/ppermute | solution.py:24
where the time goes:
time: 131 us; the launch traced here: 130 us
  starting transfers between devices  39.9 us (30%)
  other arithmetic  28.9 us (22%)
  local copies, waits for them, and re-layouts  28.2 us (22%)
  waiting for transfers between devices  19.6 us (15%)
  blocking collectives  11.9 us (9%)
    ppermute x5, starting transfers between devices, extended(): lax.ppermute(lax.slice_in_dim(block, block.shape[dim] - width, None, axis...  20.1 us
    ppermute x5, waiting for transfers between devices, extended(): lax.ppermute(lax.slice_in_dim(block, 0, width, axis=dim), axis, backward)  14 us
    unnamed x19, local copies, waits for them, and re-layouts  13.3 us
    all_to_all x1, blocking collectives, columns_settle(): lax.all_to_all(settled.reshape(shape_full), 'lev', split_axis=1, concat_a...  11.9 us
    ppermute x5, starting transfers between devices, extended(): lax.ppermute(lax.slice_in_dim(block, 0, width, axis=dim), axis, backward)  6.64 us
    ppermute x1, starting transfers between devices, passed_along(): return lax.ppermute(block, axis, route)  4.9 us
    all_to_all x1, starting transfers between devices, on_device(): lax.all_to_all(fall_speed, 'lev', split_axis=3, concat_axis=1, tiled=True)  4.13 us
    all_to_all x1, starting transfers between devices, on_device(): lax.all_to_all(field, 'lev', split_axis=3, concat_axis=1, tiled=True)  4.12 us
  transfers between devices with their start and end apart: 13, of which 8 were waited for; matrix products, arithmetic and copies ran while one was open for 19% of the time, Pallas kernels for 0%

commit v1 on v0

--- a/solution.py
+++ b/solution.py
@@ -5,6 +5,22 @@
 
 HSUB = 4
 SETTLE_SUBSTEPS = 6
+
+
+def swapped_with_each(x, axis, split, join):
+    ways, here = (lax.axis_size(axis), lax.axis_index(axis))
+    width = x.shape[split] // ways
+    shape = list(x.shape)
+    shape[split] = width
+    height = shape[join]
+    shape[join] = height * ways
+    full = jnp.zeros(shape, x.dtype)
+    for mask in range(ways):
+        part = lax.dynamic_slice_in_dim(x, (here ^ mask) * width, width, axis=split)
+        if mask:
+            part = lax.ppermute(part, axis, [(d, d ^ mask) for d in range(ways)])
+        full = lax.dynamic_update_slice_in_dim(full, part, (here ^ mask) * height, axis=join)
+    return full
 
 
 def passed_along(block, axis, distance):
@@ -126,7 +142,7 @@
         field = sweep(halo_padded_field, face_cour, 2)
     field, deposit = columns_settle(
         (
-            lax.all_to_all(field, "lev", split_axis=3, concat_axis=1, tiled=True),
+            swapped_with_each(field, "lev", 3, 1),
             lax.all_to_all(fall_speed, "lev", split_axis=3, concat_axis=1, tiled=True),
         )
     )

time: 131 us -> 121 us (0.924)
  local copies, waits for them, and re-layouts: 28.2 us -> 19.5 us
  waiting for transfers between devices: 19.6 us -> 25.6 us
  other arithmetic: 28.9 us -> 24.4 us
  starting transfers between devices: 39.9 us -> 37.2 us
    ppermute x0 -> x3, waiting for transfers between devices: none -> 10.8 us  [swapped_with_each(): part = lax.ppermute(part, axis, [(d, d ^ mask) for d in range(ways)])]
    unnamed x19 -> x17, local copies, waits for them, and re-layouts: 13.3 us -> 8.63 us
    all_to_all x1 -> x0, starting transfers between devices: 4.12 us -> none  [on_device(): lax.all_to_all(field, 'lev', split_axis=3, concat_axis=1, tiled=True)]
    all_to_all x1 -> x0, other arithmetic: 3.57 us -> none  [on_device(): lax.all_to_all(field, 'lev', split_axis=3, concat_axis=1, tiled=True)]
    all_to_all x1, waiting for transfers between devices: 3.09 us -> 0.01 us  [on_device(): lax.all_to_all(fall_speed, 'lev', split_axis=3, concat_axis=1, tiled=True)]
    ppermute x0 -> x3, starting transfers between devices: none -> 2.12 us  [swapped_with_each(): part = lax.ppermute(part, axis, [(d, d ^ mask) for d in range(ways)])]
    all_to_all x2, local copies, waits for them, and re-layouts: 2.54 us -> 0.67 us  [columns_settle(): lax.all_to_all(settled.reshape(shape_full), 'lev', split_axis=1, concat_a...]
    all_to_all x1 -> x0, waiting for transfers between devices: 1.67 us -> none  [on_device(): lax.all_to_all(field, 'lev', split_axis=3, concat_axis=1, tiled=True)]
  transfers between devices with their start and end apart: 13 -> 15, of which waited for: 8 -> 8; matrix products, arithmetic and copies ran while one was open for 19% -> 12% of each run, Pallas kernels for 0% -> 0%
where the time goes in v1:
time: 121 us; the launch traced here: 120 us
  starting transfers between devices  37.2 us (31%)
  waiting for transfers between devices  25.6 us (21%)
  other arithmetic  24.4 us (20%)
  local copies, waits for them, and re-layouts  19.5 us (16%)
  blocking collectives  11.9 us (10%)
  between operations  1.33 us (1%)
    ppermute x5, starting transfers between devices, extended(): lax.ppermute(lax.slice_in_dim(block, block.shape[dim] - width, None, axis...  20.1 us
    ppermute x5, waiting for transfers between devices, extended(): lax.ppermute(lax.slice_in_dim(block, 0, width, axis=dim), axis, backward)  14 us
    all_to_all x1, blocking collectives, columns_settle(): lax.all_to_all(settled.reshape(shape_full), 'lev', split_axis=1, concat_a...  11.9 us
    ppermute x3, waiting for transfers between devices, swapped_with_each(): part = lax.ppermute(part, axis, [(d, d ^ mask) for d in range(ways)])  10.8 us
    unnamed x17, local copies, waits for them, and re-layouts  8.63 us
    ppermute x5, starting transfers between devices, extended(): lax.ppermute(lax.slice_in_dim(block, 0, width, axis=dim), axis, backward)  6.64 us
    ppermute x1, starting transfers between devices, passed_along(): return lax.ppermute(block, axis, route)  4.9 us
    mul x12, other arithmetic, sweep(): face_flux_values = courant * jnp.where(courant >= 0, from_west, from_east)  4 us
  transfers between devices with their start and end apart: 15, of which 8 were waited for; matrix products, arithmetic and copies ran while one was open for 12% of the time, Pallas kernels for 0%

profile of v1, /device:TPU:0, one launch (start us, length us, event | category | flops | bytes accessed | tf_op | source)
XLA Modules:
  0.0 120.0 jit_solution(6517722872953652921)
XLA Ops:
  0.7 1.1 broadcast_select_fusion
  1.8 4.9 %collective-permute-start = (f32[1,1,1152]{2,1,0:T(1,128)S(1)}, f32[1,1,1152]{2,1,0:T(1,128)S(1)}, u32[]{:S(2)}, u32[]{:S(2)}) collective-permute-start(f32[1,1,1152]{2,1,0:T(1,128)S(1)} %slice.704), channel_id=1, source_target_pairs={{0,4},{4,8},{8,12},{12,16},{16,20},{20,24},{24,28},{1,5},{5,9},{9,... | collective-permute-start | bytes 13832 | tf_op jit(solution)/shard_map/ppermute | solution.py:29
  7.5 1.1 fusion.142
  8.6 1.1 abs_multiply_fusion.1
  11.6 3.4 %collective-permute-start.1 = (f32[2,1,3,1152]{3,2,0,1:T(4,128)S(1)}, f32[2,1,3,1152]{3,2,0,1:T(4,128)S(1)}, u32[]{:S(2)}, u32[]{:S(2)}) collective-permute-start(f32[2,1,3,1152]{3,2,0,1:T(4,128)S(1)} %get-tuple-element.49), channel_id=1, source_target_pairs={{0,4},{4,8},{8,12},{12,16},{16,20},{20,24},{24,28},{1,5},{5,9},{9,... | collective-permute-start | bytes 82952 | tf_op jit(solution)/shard_map/ppermute | solution.py:37
  15.1 1.3 %collective-permute-start.2 = (f32[2,1,3,1152]{3,2,0,1:T(4,128)S(1)}, f32[2,1,3,1152]{3,2,0,1:T(4,128)S(1)}, u32[]{:S(2)}, u32[]{:S(2)}) collective-permute-start(f32[2,1,3,1152]{3,2,0,1:T(4,128)S(1)} %get-tuple-element.50), channel_id=1, source_target_pairs={{4,0},{8,4},{12,8},{16,12},{20,16},{24,20},{28,24},{5,1},{9,5},{13... | collective-permute-start | bytes 82952 | tf_op jit(solution)/shard_map/ppermute | solution.py:40
  16.7 4.2 %collective-permute-done.2 = f32[2,1,3,1152]{3,2,0,1:T(4,128)S(1)} collective-permute-done((f32[2,1,3,1152]{3,2,0,1:T(4,128)S(1)}, f32[2,1,3,1152]{3,2,0,1:T(4,128)S(1)}, u32[]{:S(2)}, u32[]{:S(2)}) %collective-permute-start.2) | collective-permute-done | bytes 27680 | tf_op jit(solution)/shard_map/ppermute | solution.py:40
  23.7 4.3 %collective-permute-start.3 = (f32[2,1,3,1152]{3,2,0,1:T(4,128)S(1)}, f32[2,1,3,1152]{3,2,0,1:T(4,128)S(1)}, u32[]{:S(2)}, u32[]{:S(2)}) collective-permute-start(f32[2,1,3,1152]{3,2,0,1:T(4,128)S(1)} %get-tuple-element.45), channel_id=1, source_target_pairs={{0,4},{4,8},{8,12},{12,16},{16,20},{20,24},{24,28},{1,5},{5,9},{9,... | collective-permute-start | bytes 82952 | tf_op jit(solution)/shard_map/ppermute | solution.py:37
  28.0 1.3 %collective-permute-start.4 = (f32[2,1,3,1152]{3,2,0,1:T(4,128)S(1)}, f32[2,1,3,1152]{3,2,0,1:T(4,128)S(1)}, u32[]{:S(2)}, u32[]{:S(2)}) collective-permute-start(f32[2,1,3,1152]{3,2,0,1:T(4,128)S(1)} %get-tuple-element.46), channel_id=1, source_target_pairs={{4,0},{8,4},{12,8},{16,12},{20,16},{24,20},{28,24},{5,1},{9,5},{13... | collective-permute-start | bytes 82952 | tf_op jit(solution)/shard_map/ppermute | solution.py:40
  29.6 4.2 %collective-permute-done.4 = f32[2,1,3,1152]{3,2,0,1:T(4,128)S(1)} collective-permute-done((f32[2,1,3,1152]{3,2,0,1:T(4,128)S(1)}, f32[2,1,3,1152]{3,2,0,1:T(4,128)S(1)}, u32[]{:S(2)}, u32[]{:S(2)}) %collective-permute-start.4) | collective-permute-done | bytes 27680 | tf_op jit(solution)/shard_map/ppermute | solution.py:40
  36.6 3.4 %collective-permute-start.5 = (f32[2,1,3,1152]{3,2,0,1:T(4,128)S(1)}, f32[2,1,3,1152]{3,2,0,1:T(4,128)S(1)}, u32[]{:S(2)}, u32[]{:S(2)}) collective-permute-start(f32[2,1,3,1152]{3,2,0,1:T(4,128)S(1)} %get-tuple-element.41), channel_id=1, source_target_pairs={{0,4},{4,8},{8,12},{12,16},{16,20},{20,24},{24,28},{1,5},{5,9},{9,... | collective-permute-start | bytes 82952 | tf_op jit(solution)/shard_map/ppermute | solution.py:37
  40.0 1.3 %collective-permute-start.6 = (f32[2,1,3,1152]{3,2,0,1:T(4,128)S(1)}, f32[2,1,3,1152]{3,2,0,1:T(4,128)S(1)}, u32[]{:S(2)}, u32[]{:S(2)}) collective-permute-start(f32[2,1,3,1152]{3,2,0,1:T(4,128)S(1)} %get-tuple-element.42), channel_id=1, source_target_pairs={{4,0},{8,4},{12,8},{16,12},{20,16},{24,20},{28,24},{5,1},{9,5},{13... | collective-permute-start | bytes 82952 | tf_op jit(solution)/shard_map/ppermute | solution.py:40
  41.8 4.1 %collective-permute-done.6 = f32[2,1,3,1152]{3,2,0,1:T(4,128)S(1)} collective-permute-done((f32[2,1,3,1152]{3,2,0,1:T(4,128)S(1)}, f32[2,1,3,1152]{3,2,0,1:T(4,128)S(1)}, u32[]{:S(2)}, u32[]{:S(2)}) %collective-permute-start.6) | collective-permute-done | bytes 27680 | tf_op jit(solution)/shard_map/ppermute | solution.py:40
  48.6 4.3 %collective-permute-start.7 = (f32[2,1,3,1152]{3,2,0,1:T(4,128)S(1)}, f32[2,1,3,1152]{3,2,0,1:T(4,128)S(1)}, u32[]{:S(2)}, u32[]{:S(2)}) collective-permute-start(f32[2,1,3,1152]{3,2,0,1:T(4,128)S(1)} %get-tuple-element.37), channel_id=1, source_target_pairs={{0,4},{4,8},{8,12},{12,16},{16,20},{20,24},{24,28},{1,5},{5,9},{9,... | collective-permute-start | bytes 82952 | tf_op jit(solution)/shard_map/ppermute | solution.py:37
  52.9 1.5 %collective-permute-start.8 = (f32[2,1,3,1152]{3,2,0,1:T(4,128)S(1)}, f32[2,1,3,1152]{3,2,0,1:T(4,128)S(1)}, u32[]{:S(2)}, u32[]{:S(2)}) collective-permute-start(f32[2,1,3,1152]{3,2,0,1:T(4,128)S(1)} %get-tuple-element.38), channel_id=1, source_target_pairs={{4,0},{8,4},{12,8},{16,12},{20,16},{24,20},{28,24},{5,1},{9,5},{13... | collective-permute-start | bytes 82952 | tf_op jit(solution)/shard_map/ppermute | solution.py:40
  54.4 2.0 %copy.47 = f32[2,1,48,1152]{2,0,1,3:T(2,128)S(1)} copy(f32[2,1,48,1152]{3,2,1,0:T(8,128)} %param.7) | data formatting | bytes 884736 | tf_op args[3]
  56.4 2.9 %reshape.593 = f32[4,1,27648]{2,1,0:T(1,128)} reshape(f32[1152,1,2,48]{3,2,1,0:T(2,128)S(1)} %bitcast.44) | data formatting | bytes 884736
  59.2 3.5 %all-to-all-start = ((f32[4,1,27648]{2,1,0:T(1,128)}), f32[4,1,27648]{2,1,0:T(1,128)S(1)}, u32[]{:S(2)}, u32[]{:S(2)}) async-start(f32[4,1,27648]{2,1,0:T(1,128)} %reshape.593), calls=%async_computation | async-start | bytes 884736 | tf_op jit(solution)/shard_map/all_to_all | solution.py:146
  63.9 1.7 %collective-permute-start.11 = (f32[2,1,48,288]{3,2,0,1:T(8,128)S(1)}, f32[2,1,48,288]{3,2,0,1:T(8,128)S(1)}, u32[]{:S(2)}, u32[]{:S(2)}) collective-permute-start(f32[2,1,48,288]{3,2,0,1:T(8,128)S(1)} %get-tuple-element.34), channel_id=1, source_target_pairs={{0,3},{1,2},{2,1},{3,0},{4,7},{5,6},{6,5},{7,4},{8,11},{9,10},{10,... | collective-permute-start | bytes 331784 | tf_op jit(solution)/shard_map/ppermute | solution.py:21
  66.2 1.2 %collective-permute-done.9 = f32[2,1,48,288]{3,2,0,1:T(8,128)S(1)} collective-permute-done((f32[2,1,48,288]{3,2,0,1:T(8,128)S(1)}, f32[2,1,48,288]{3,2,0,1:T(8,128)S(1)}, u32[]{:S(2)}, u32[]{:S(2)}) %collective-permute-start.9) | collective-permute-done | bytes 110624 | tf_op jit(solution)/shard_map/ppermute | solution.py:21
  67.4 9.6 %collective-permute-done.10 = f32[2,1,48,288]{3,2,0,1:T(8,128)S(1)} collective-permute-done((f32[2,1,48,288]{3,2,0,1:T(8,128)S(1)}, f32[2,1,48,288]{3,2,0,1:T(8,128)S(1)}, u32[]{:S(2)}, u32[]{:S(2)}) %collective-permute-start.10) | collective-permute-done | bytes 110624 | tf_op jit(solution)/shard_map/ppermute | solution.py:21
  78.0 1.9 %reduce.2 = f32[4,27648]{1,0:T(4,128)S(1)} reduce(f32[4,1,27648]{2,1,0:T(1,128)S(1)} %all-to-all-done, f32[]{:T(128)} %broadcast.305), dimensions={1}, to_apply=%all_to_all.24.reduce_sub_computation | reduce | bytes 884740 | tf_op jit(solution)/shard_map/all_to_all | solution.py:146
  79.9 3.0 %reshape.594 = f32[1152,1,2,48]{3,2,1,0:T(2,128)} reshape(f32[4,27648]{1,0:T(4,128)S(1)} %reduce.2) | data formatting | bytes 884736
  82.9 1.6 %copy.48 = f32[2,1,48,4,288]{4,2,3,0,1:T(8,128)S(1)} copy(f32[2,1,48,4,288]{2,0,4,3,1:T(2,128)} %bitcast.43) | data formatting | bytes 884736 | tf_op jit(solution)/shard_map/all_to_all | solution.py:146
  88.8 1.3 %add_subtract_fusion = f32[2,4,13824]{2,1,0:T(4,128)} fusion(f32[2,3,13824]{2,1,0:T(4,128)S(1)} %bitcast.58, f32[2,4,13824]{2,1,0:T(4,128)S(1)} %get-tuple-element.7, f32[2,3,13824]{2,1,0:T(4,128)S(1)} %bitcast.50, f32[2,4,13824]{2,1,0:T(4,128)S(1)} %reshape.589), kind=kLoop, calls=%fused_computation.206 | loop fusion | flops 1327104 | bytes 1990656 | tf_op jit(solution)/shard_map/sub | solution.py:112
  90.1 2.3 %reshape.590 = f32[2,4,48,288]{3,2,1,0:T(8,128)} reshape(f32[2,4,13824]{2,1,0:T(4,128)} %add_subtract_fusion) | data formatting | bytes 884736 | tf_op jit(solution)/shard_map/reshape | solution.py:123
  92.4 1.1 copy.49
  93.5 11.9 %all_to_all.33 = f32[2,4,48,288]{3,2,0,1:T(8,128)S(1)} all-to-all(f32[2,4,48,288]{3,2,0,1:T(8,128)S(1)} %copy.49), channel_id=1, replica_groups=mesh['lat'=8,'lev'=4] {'lev'}, dimensions={1} | all-to-all | bytes 884736 | tf_op jit(solution)/shard_map/all_to_all | solution.py:122
  107.9 4.5 %collective-permute-start.12 = (f32[2,1,3,1152]{3,2,0,1:T(4,128)S(1)}, f32[2,1,3,1152]{3,2,0,1:T(4,128)S(1)}, u32[]{:S(2)}, u32[]{:S(2)}) collective-permute-start(f32[2,1,3,1152]{3,2,0,1:T(4,128)S(1)} %get-tuple-element.30), channel_id=1, source_target_pairs={{0,4},{4,8},{8,12},{12,16},{16,20},{20,24},{24,28},{1,5},{5,9},{9,... | collective-permute-start | bytes 82952 | tf_op jit(solution)/shard_map/ppermute | solution.py:37
  112.5 1.3 %collective-permute-start.13 = (f32[2,1,3,1152]{3,2,0,1:T(4,128)S(1)}, f32[2,1,3,1152]{3,2,0,1:T(4,128)S(1)}, u32[]{:S(2)}, u32[]{:S(2)}) collective-permute-start(f32[2,1,3,1152]{3,2,0,1:T(4,128)S(1)} %get-tuple-element.31), channel_id=1, source_target_pairs={{4,0},{8,4},{12,8},{16,12},{20,16},{24,20},{28,24},{5,1},{9,5},{13... | collective-permute-start | bytes 82952 | tf_op jit(solution)/shard_map/ppermute | solution.py:40
  113.8 2.3 %fusion.143 = f32[2,13824]{1,0:T(2,128)S(1)} fusion(f32[2,4,13824]{2,1,0:T(4,128)} %copy-done.4, f32[2,4,13824]{2,1,0:T(4,128)} %copy-done, f32[2,4,13824]{2,1,0:T(4,128)} %copy-done.3, f32[2,4,13824]{2,1,0:T(4,128)S(1)} %get-tuple-element.8, f32[2,4,13824]{2,1,0:T(4,128)} %copy-done.2, f32[2,4,13824]{2,1,0:T(4,128)S(1)} %multiply_multiply_fusion.5), kind=kLoop, calls=%fused_computation.233 | loop fusion | flops 138240 | bytes 774144 | tf_op jit(solution)/shard_map/add | solution.py:113
  116.9 1.4 %collective-permute-done.13 = f32[2,1,3,1152]{3,2,0,1:T(4,128)S(1)} collective-permute-done((f32[2,1,3,1152]{3,2,0,1:T(4,128)S(1)}, f32[2,1,3,1152]{3,2,0,1:T(4,128)S(1)}, u32[]{:S(2)}, u32[]{:S(2)}) %collective-permute-start.13) | collective-permute-done | bytes 27680 | tf_op jit(solution)/shard_map/ppermute | solution.py:40
  (111 shorter events, 23.7 us)
Async XLA Ops:
  0.6 9.1 %copy-start.5 = (f32[1,48,1152]{2,1,0:T(8,128)S(1)}, f32[1,48,1152]{2,1,0:T(8,128)}, u32[]{:S(2)}) copy-start(f32[1,48,1152]{2,1,0:T(8,128)} %param.5) | copy-start | bytes 663556
  0.6 9.0 %copy-start.1 = (f32[2,1,48,1152]{3,2,1,0:T(8,128)S(1)}, f32[2,1,48,1152]{3,2,1,0:T(8,128)}, u32[]{:S(2)}) copy-start(f32[2,1,48,1152]{3,2,1,0:T(8,128)} %param.4) | copy-start | bytes 1327108
  1.8 14.7 %collective-permute-start = (f32[1,1,1152]{2,1,0:T(1,128)S(1)}, f32[1,1,1152]{2,1,0:T(1,128)S(1)}, u32[]{:S(2)}, u32[]{:S(2)}) collective-permute-start(f32[1,1,1152]{2,1,0:T(1,128)S(1)} %slice.704), channel_id=1, source_target_pairs={{0,4},{4,8},{8,12},{12,16},{16,20},{20,24},{24,28},{1,5},{5,9},{9,... | collective-permute-start | bytes 13832 | tf_op jit(solution)/shard_map/ppermute | solution.py:29
  11.4 5.0 %copy-start.6 = (f32[1,48,1152]{2,1,0:T(8,128)S(1)}, f32[1,48,1152]{2,1,0:T(8,128)}, u32[]{:S(2)}) copy-start(f32[1,48,1152]{2,1,0:T(8,128)} %param.6) | copy-start | bytes 663556
  11.6 5.1 %collective-permute-start.1 = (f32[2,1,3,1152]{3,2,0,1:T(4,128)S(1)}, f32[2,1,3,1152]{3,2,0,1:T(4,128)S(1)}, u32[]{:S(2)}, u32[]{:S(2)}) collective-permute-start(f32[2,1,3,1152]{3,2,0,1:T(4,128)S(1)} %get-tuple-element.49), channel_id=1, source_target_pairs={{0,4},{4,8},{8,12},{12,16},{16,20},{20,24},{24,28},{1,5},{5,9},{9,... | collective-permute-start | bytes 82952 | tf_op jit(solution)/shard_map/ppermute | solution.py:37
  15.1 5.9 %collective-permute-start.2 = (f32[2,1,3,1152]{3,2,0,1:T(4,128)S(1)}, f32[2,1,3,1152]{3,2,0,1:T(4,128)S(1)}, u32[]{:S(2)}, u32[]{:S(2)}) collective-permute-start(f32[2,1,3,1152]{3,2,0,1:T(4,128)S(1)} %get-tuple-element.50), channel_id=1, source_target_pairs={{4,0},{8,4},{12,8},{16,12},{20,16},{24,20},{28,24},{5,1},{9,5},{13... | collective-permute-start | bytes 82952 | tf_op jit(solution)/shard_map/ppermute | solution.py:40
  23.7 6.0 %collective-permute-start.3 = (f32[2,1,3,1152]{3,2,0,1:T(4,128)S(1)}, f32[2,1,3,1152]{3,2,0,1:T(4,128)S(1)}, u32[]{:S(2)}, u32[]{:S(2)}) collective-permute-start(f32[2,1,3,1152]{3,2,0,1:T(4,128)S(1)} %get-tuple-element.45), channel_id=1, source_target_pairs={{0,4},{4,8},{8,12},{12,16},{16,20},{20,24},{24,28},{1,5},{5,9},{9,... | collective-permute-start | bytes 82952 | tf_op jit(solution)/shard_map/ppermute | solution.py:37
  28.0 5.9 %collective-permute-start.4 = (f32[2,1,3,1152]{3,2,0,1:T(4,128)S(1)}, f32[2,1,3,1152]{3,2,0,1:T(4,128)S(1)}, u32[]{:S(2)}, u32[]{:S(2)}) collective-permute-start(f32[2,1,3,1152]{3,2,0,1:T(4,128)S(1)} %get-tuple-element.46), channel_id=1, source_target_pairs={{4,0},{8,4},{12,8},{16,12},{20,16},{24,20},{28,24},{5,1},{9,5},{13... | collective-permute-start | bytes 82952 | tf_op jit(solution)/shard_map/ppermute | solution.py:40
  36.6 5.2 %collective-permute-start.5 = (f32[2,1,3,1152]{3,2,0,1:T(4,128)S(1)}, f32[2,1,3,1152]{3,2,0,1:T(4,128)S(1)}, u32[]{:S(2)}, u32[]{:S(2)}) collective-permute-start(f32[2,1,3,1152]{3,2,0,1:T(4,128)S(1)} %get-tuple-element.41), channel_id=1, source_target_pairs={{0,4},{4,8},{8,12},{12,16},{16,20},{20,24},{24,28},{1,5},{5,9},{9,... | collective-permute-start | bytes 82952 | tf_op jit(solution)/shard_map/ppermute | solution.py:37
  40.0 5.9 %collective-permute-start.6 = (f32[2,1,3,1152]{3,2,0,1:T(4,128)S(1)}, f32[2,1,3,1152]{3,2,0,1:T(4,128)S(1)}, u32[]{:S(2)}, u32[]{:S(2)}) collective-permute-start(f32[2,1,3,1152]{3,2,0,1:T(4,128)S(1)} %get-tuple-element.42), channel_id=1, source_target_pairs={{4,0},{8,4},{12,8},{16,12},{20,16},{24,20},{28,24},{5,1},{9,5},{13... | collective-permute-start | bytes 82952 | tf_op jit(solution)/shard_map/ppermute | solution.py:40
  48.6 14.2 %collective-permute-start.7 = (f32[2,1,3,1152]{3,2,0,1:T(4,128)S(1)}, f32[2,1,3,1152]{3,2,0,1:T(4,128)S(1)}, u32[]{:S(2)}, u32[]{:S(2)}) collective-permute-start(f32[2,1,3,1152]{3,2,0,1:T(4,128)S(1)} %get-tuple-element.37), channel_id=1, source_target_pairs={{0,4},{4,8},{8,12},{12,16},{16,20},{20,24},{24,28},{1,5},{5,9},{9,... | collective-permute-start | bytes 82952 | tf_op jit(solution)/shard_map/ppermute | solution.py:37
  52.9 9.8 %collective-permute-start.8 = (f32[2,1,3,1152]{3,2,0,1:T(4,128)S(1)}, f32[2,1,3,1152]{3,2,0,1:T(4,128)S(1)}, u32[]{:S(2)}, u32[]{:S(2)}) collective-permute-start(f32[2,1,3,1152]{3,2,0,1:T(4,128)S(1)} %get-tuple-element.38), channel_id=1, source_target_pairs={{4,0},{8,4},{12,8},{16,12},{20,16},{24,20},{28,24},{5,1},{9,5},{13... | collective-permute-start | bytes 82952 | tf_op jit(solution)/shard_map/ppermute | solution.py:40
  59.2 18.2 %all-to-all-start = ((f32[4,1,27648]{2,1,0:T(1,128)}), f32[4,1,27648]{2,1,0:T(1,128)S(1)}, u32[]{:S(2)}, u32[]{:S(2)}) async-start(f32[4,1,27648]{2,1,0:T(1,128)} %reshape.593), calls=%async_computation | async-start | bytes 884736 | tf_op jit(solution)/shard_map/all_to_all | solution.py:146
  63.9 13.1 %collective-permute-start.11 = (f32[2,1,48,288]{3,2,0,1:T(8,128)S(1)}, f32[2,1,48,288]{3,2,0,1:T(8,128)S(1)}, u32[]{:S(2)}, u32[]{:S(2)}) collective-permute-start(f32[2,1,48,288]{3,2,0,1:T(8,128)S(1)} %get-tuple-element.34), channel_id=1, source_target_pairs={{0,3},{1,2},{2,1},{3,0},{4,7},{5,6},{6,5},{7,4},{8,11},{9,10},{10,... | collective-permute-start | bytes 331784 | tf_op jit(solution)/shard_map/ppermute | solution.py:21
  65.6 11.3 %collective-permute-start.10 = (f32[2,1,48,288]{3,2,0,1:T(8,128)S(1)}, f32[2,1,48,288]{3,2,0,1:T(8,128)S(1)}, u32[]{:S(2)}, u32[]{:S(2)}) collective-permute-start(f32[2,1,48,288]{3,2,0,1:T(8,128)S(1)} %get-tuple-element.35), channel_id=1, source_target_pairs={{0,2},{1,3},{2,0},{3,1},{4,6},{5,7},{6,4},{7,5},{8,10},{9,11},{10,... | collective-permute-start | bytes 331784 | tf_op jit(solution)/shard_map/ppermute | solution.py:21
  66.0 1.4 %collective-permute-start.9 = (f32[2,1,48,288]{3,2,0,1:T(8,128)S(1)}, f32[2,1,48,288]{3,2,0,1:T(8,128)S(1)}, u32[]{:S(2)}, u32[]{:S(2)}) collective-permute-start(f32[2,1,48,288]{3,2,0,1:T(8,128)S(1)} %get-tuple-element.36), channel_id=1, source_target_pairs={{0,1},{1,0},{2,3},{3,2},{4,5},{5,4},{6,7},{7,6},{8,9},{9,8},{10,11... | collective-permute-start | bytes 331784 | tf_op jit(solution)/shard_map/ppermute | solution.py:21
  85.5 0.8 copy-start.2
  86.8 0.8 copy-start.3
  87.5 2.6 %copy-start = (f32[2,4,13824]{2,1,0:T(4,128)}, f32[2,4,13824]{2,1,0:T(4,128)S(1)}, u32[]{:S(2)}) copy-start(f32[2,4,13824]{2,1,0:T(4,128)S(1)} %get-tuple-element.6) | copy-start | bytes 1327108
  88.0 0.8 copy-start.4
  107.9 9.0 %collective-permute-start.12 = (f32[2,1,3,1152]{3,2,0,1:T(4,128)S(1)}, f32[2,1,3,1152]{3,2,0,1:T(4,128)S(1)}, u32[]{:S(2)}, u32[]{:S(2)}) collective-permute-start(f32[2,1,3,1152]{3,2,0,1:T(4,128)S(1)} %get-tuple-element.30), channel_id=1, source_target_pairs={{0,4},{4,8},{8,12},{12,16},{16,20},{20,24},{24,28},{1,5},{5,9},{9,... | collective-permute-start | bytes 82952 | tf_op jit(solution)/shard_map/ppermute | solution.py:37
  112.5 5.9 %collective-permute-start.13 = (f32[2,1,3,1152]{3,2,0,1:T(4,128)S(1)}, f32[2,1,3,1152]{3,2,0,1:T(4,128)S(1)}, u32[]{:S(2)}, u32[]{:S(2)}) collective-permute-start(f32[2,1,3,1152]{3,2,0,1:T(4,128)S(1)} %get-tuple-element.31), channel_id=1, source_target_pairs={{4,0},{8,4},{12,8},{16,12},{20,16},{24,20},{28,24},{5,1},{9,5},{13... | collective-permute-start | bytes 82952 | tf_op jit(solution)/shard_map/ppermute | solution.py:40
